TPU v7x, 256 devices: a whole 4x4x8 slice. The times are simulated.
256 devices in a mesh: row: 64 (over x, y_lo, z), panel: 4 (over y_hi, core).
Axes of the slice: x: 4, y: 4 (y_hi: 2, y_lo: 2; y = y_hi * 2 + y_lo), z: 8, core: 2. Of those that a mesh axis runs over, the one named last changes fastest.
Arguments:
- pixel_ids: int32 [65536], P('row'), may hold values from 0 to 65535, each once
- quad_offsets: int32 [2, 16, 65536], P(None, None, 'row'), may hold values from 0 to 7
- prior_factor: float32 [65536, 2048], P('row', 'panel'), may hold values from -0.036 to 0.036, as said below
Outputs:
- panel_factor: float32 [65536, 1024], P(('row', 'panel'))
Inputs may be any that keep to these rules, and one draw needn't show every extreme that they name: `pixel_ids`: each pixel of the grid appears in exactly one row. `prior_factor`: schur[panel_index] is positive definite.
All inputs are finite; a program needn't handle non-finite values.
Results may differ from a plain program's by a relative error of at most 0.0003.
Values sent between devices are 32-bit elements; how exact they have to be, the bound alone decides.
A program may use at most 128 MiB of HBM per device.

v0:
```python
import jax
import jax.numpy as jnp
from jax import lax
from jax.sharding import PartitionSpec as P

B = 1024
range_inverse = 1.0


def from_behind(block, axis, distance):
    devices = range(lax.axis_size(axis))
    route = [((i - distance) % len(devices), i) for i in devices]
    return lax.ppermute(block, axis, route)


def locate(pixel_ids, quad_offsets):
    column = (pixel_ids % 256).astype(jnp.float32)
    lines = (pixel_ids // 256).astype(jnp.float32)
    east = column[None, :] + (quad_offsets[0].astype(jnp.float32) + 0.5) / 8.0
    north = lines[None, :] + (quad_offsets[1].astype(jnp.float32) + 0.5) / 8.0
    return (east, north)


def cover_tile(east_rows, north_rows, east_cols, north_cols):
    count = east_rows.shape[0]

    def accumulate(index, running):
        east_one = lax.dynamic_index_in_dim(east_rows, index, 0, keepdims=False)
        north_one = lax.dynamic_index_in_dim(north_rows, index, 0, keepdims=False)
        apart_east = east_cols[:, :, None] - east_one[None, None, :]
        apart_north = north_cols[:, :, None] - north_one[None, None, :]
        return running + jnp.sum(
            jnp.exp(-(apart_east * apart_east + apart_north * apart_north) * range_inverse), axis=0
        )

    start = jnp.zeros((east_cols.shape[1], east_rows.shape[1]), jnp.float32)
    total = lax.fori_loop(0, count, accumulate, start)
    return total.T / float(count * count)


def local(pixel_ids, quad_offsets, prior_factor):
    panel_count = lax.axis_size("panel")
    row_count = lax.axis_size("row")
    block_rows = pixel_ids.shape[0]
    quarter_rows = block_rows // panel_count
    per_device = B // (row_count * panel_count)
    span_cols = panel_count * per_device
    row_pos = lax.axis_index("row")
    panel_pos = lax.axis_index("panel")
    east, north = locate(pixel_ids, quad_offsets)
    all_points = jnp.stack([east, north])
    own_points = lax.dynamic_slice_in_dim(all_points, panel_pos * quarter_rows, quarter_rows, 2)
    own_east = own_points[0]
    own_north = own_points[1]
    local_points = all_points.reshape(2, east.shape[0], panel_count, quarter_rows)[
        :, :, :, :per_device
    ]
    local_points = local_points.reshape(2, east.shape[0], span_cols)
    start_cols = jnp.zeros((quarter_rows, B), jnp.float32)

    def place(columns, held, source):
        tile = cover_tile(own_east, own_north, held[0], held[1])
        return lax.dynamic_update_slice(columns, tile, (jnp.int32(0), source * span_cols))

    def turn(index, carry):
        held, columns = carry
        columns = place(columns, held, (row_pos - index) % row_count)
        held = from_behind(held, "row", 1)
        return (held, columns)

    held, columns = lax.fori_loop(0, row_count - 1, turn, (local_points, start_cols))
    columns = place(columns, held, (row_pos - (row_count - 1)) % row_count)
    device_pos = row_pos * panel_count + panel_pos
    row_ids = jnp.arange(quarter_rows, dtype=jnp.int32)[:, None]
    col_ids = jnp.arange(B, dtype=jnp.int32)[None, :]
    on_diagonal = (row_ids < per_device) & (col_ids == device_pos * per_device + row_ids)
    cover = columns + jnp.where(on_diagonal, 1.0, 0.0).astype(jnp.float32)
    whole_rows = lax.all_to_all(prior_factor, "panel", split_axis=0, concat_axis=1, tiled=True)
    panel_prior = lax.all_gather(whole_rows[:per_device], ("row", "panel"), axis=0, tiled=True)
    update = jnp.dot(
        whole_rows,
        panel_prior.T,
        precision=lax.Precision.HIGHEST,
        preferred_element_type=jnp.float32,
    )
    schur = cover - update
    diag_rows = lax.all_gather(schur[:per_device], ("row", "panel"), axis=0, tiled=True)
    diag_factor = jnp.linalg.cholesky(diag_rows)
    return lax.linalg.triangular_solve(
        diag_factor, schur, left_side=False, lower=True, transpose_a=True
    )


def solution(mesh):
    return jax.shard_map(
        local,
        mesh=mesh,
        in_specs=(P("row"), P(None, None, "row"), P("row", "panel")),
        out_specs=P(("row", "panel"), None),
        check_vma=False,
    )
```

profile of v0, /device:TPU:32, one launch (start us, length us, event | category | flops | bytes accessed | tf_op | source)
XLA Modules:
  0.0 1338.7 jit_solution(4955843680710674743)
XLA Ops:
  11.4 26.9 %all-to-all-done = f32[4,256,512]{2,1,0:T(8,128)S(1)} async-done(((f32[4,256,512]{2,1,0:T(8,128)}), f32[4,256,512]{2,1,0:T(8,128)S(1)}, u32[]{:S(2)}, u32[]{:S(2)}) %all-to-all-start) | async-done | bytes 2097184 | tf_op jit(solution)/shard_map/all_to_all | solution.py:78
  39.1 497.6 %while.68 = (s32[]{:T(128)}, f32[2,16,16]{2,1,0:T(8,128)S(1)}, f32[256,1024]{0,1:T(8,128)S(1)}, f32[16,256]{1,0:T(8,128)S(1)}, f32[16,256]{1,0:T(8,128)S(1)}, /*...) while((s32[]{:T(128)}, f32[2,16,16]{2,1,0:T(8,128)S(1)}, ...), condition=%wide.region_4.5_spmd, body=%wide.region_0.4_spmd.sunk | while | flops 466965 | bytes 123403 | solution.py:71
  545.9 10.2 reshape.138
  556.0 16.1 %convolution_subtract_fusion = f32[256,1024]{1,0:T(8,128)S(1)} fusion(f32[256,2048]{0,1:T(8,128)S(1)} %bitcast.152, f32[1024,2048]{1,0:T(8,128)} %reshape.138, f32[256,1024]{1,0:T(8,128)S(1)} %dynamic_update_slice.13, s32[256]{0:T(256)S(1)} %iota_add_fusion, pred[256]{0:T(512)(128)(4,1)S(1)} %iota_compare_fusion.4), kind=kOutput, calls=%fused_computation.15 | convolution fusion | flops 6443761664 | bytes 12584192 | tf_op jit(solution)/shard_map/dot_general | solution.py:80
  573.7 412.5 %all-gather.7.cloned.1.call-done = f32[256,4,1024]{2,1,0:T(4,128)} async-done(((f32[1,4,1024]{2,1,0:T(4,128)}), f32[256,4,1024]{2,1,0:T(4,128)}) %all-gather.7.cloned.1.call-update) | async-done | bytes 4194320 | tf_op jit(solution)/shard_map/all_gather | solution.py:87
  986.2 5.3 reshape.140
  991.5 5.8 copy.69
  1003.6 11.7 cholesky.223
  1017.9 9.8 custom-call.62
  1031.6 11.9 cholesky.244
  1044.2 9.8 custom-call.63
  1057.3 11.7 cholesky.468
  1069.7 9.8 custom-call.64
  1083.0 11.9 cholesky.487
  1095.5 9.8 custom-call.65
  1108.8 11.7 cholesky.506
  1121.2 10.2 custom-call.66
  1134.7 11.7 cholesky.526
  1147.0 9.8 custom-call.67
  1159.8 11.7 cholesky.546
  1172.2 9.8 custom-call.68
  1184.6 11.7 cholesky.564
  1212.2 22.8 %while.69 = (s32[]{:T(128)}, f32[1024,1024]{1,0:T(8,128)}, s32[8,2]{0,1:T(2,128)S(1)}, f32[8,128,128]{2,1,0:T(8,128)S(1)}, s32[]{:T(128)}) while((s32[]{:T(128)}, f32[1024,1024]{1,0:T(8,128)}, s32[8,2]{0,1:T(2,128)S(1)}, f32[8,128,128]{2,1,0:T(8,128)S(1)}, s32[]{:T(128)}) %tuple.176), condition=%wide.while_cond, body=%wide.while_body.sunk | while | flops 2 | bytes 131189 | solution.py:89
  1235.1 78.8 %custom-call.69 = f32[8,128,128]{1,2,0:T(8,128)S(1)} custom-call(f32[8,128,128]{2,1,0:T(8,128)S(1)} %get-tuple-element.405), custom_call_target="InvertDiagBlocksLowerTriangular" | custom-call | tf_op jit(solution)/shard_map/triangular_solve | solution.py:89
  (3637 shorter events, 763.7 us)
Async XLA Ops:
  6.5 31.8 %all-to-all-start = ((f32[4,256,512]{2,1,0:T(8,128)}), f32[4,256,512]{2,1,0:T(8,128)S(1)}, u32[]{:S(2)}, u32[]{:S(2)}) async-start(f32[4,256,512]{2,1,0:T(8,128)} %bitcast.153), calls=%async_computation | async-start | bytes 4194304 | tf_op jit(solution)/shard_map/all_to_all | solution.py:78
  11.1 534.7 %all-gather.5.cloned.1.call-start = ((), (), s32[]{:S(2)}) async-start(), calls=%async_computation.1 | async-start | bytes 8421376 | tf_op jit(solution)/shard_map/all_gather | solution.py:79
  39.0 947.2 %all-gather.7.cloned.1.call-start = ((), (), s32[]{:S(2)}) async-start(), calls=%async_computation.2 | async-start | bytes 4210688 | tf_op jit(solution)/shard_map/all_gather | solution.py:87
  58.9 8.0 collective-permute-start
  66.8 8.0 collective-permute-start
  74.9 8.0 collective-permute-start
  82.9 8.1 collective-permute-start
  98.8 8.0 collective-permute-start
  114.8 8.0 collective-permute-start
  122.7 8.0 collective-permute-start
  130.7 8.0 collective-permute-start
  162.5 8.0 collective-permute-start
  186.4 8.0 collective-permute-start
  194.4 8.0 collective-permute-start
  218.3 8.0 collective-permute-start
  234.2 8.0 collective-permute-start
  250.1 8.0 collective-permute-start
  274.0 8.0 collective-permute-start
  305.8 8.0 collective-permute-start
  329.7 8.0 collective-permute-start
  345.6 8.0 collective-permute-start
  393.4 8.0 collective-permute-start
  465.1 8.0 collective-permute-start
  496.9 8.0 collective-permute-start
  (49 other events, 459.4 us)
Sparse Core Ops, SparseCore 0:
  39.1 420.7 all-gather.4
  573.8 412.3 all-gather.6
where the time goes:
time: 1350 us; the launch traced here: 1340 us
  waiting for transfers between devices  722 us (53%)
  other arithmetic  416 us (31%)
  local copies, waits for them, and re-layouts  69 us (5%)
  matrix products  55.5 us (4%)
  loops' own time  45.9 us (3%)
  between operations  19.1 us (1%)
    all_gather x1, waiting for transfers between devices, local(): lax.all_gather(schur[:per_device], ('row', 'panel'), axis=0, tiled=True)  412 us
    ppermute x63, waiting for transfers between devices, from_behind(): return lax.ppermute(block, axis, route)  283 us
    another operation x31, other arithmetic, local(): diag_factor = jnp.linalg.cholesky(diag_rows)  173 us
    reduce_sum x1024, other arithmetic, accumulate(): jnp.sum(jnp.exp(-(apart_east * apart_east + apart_north * apart_north) *...  148 us
    another operation x3, other arithmetic, local(): lax.linalg.triangular_solve(diag_factor, schur, left_side=False, lower=Tr...  83.7 us
    another operation x64, loops' own time, cover_tile(): total = lax.fori_loop(0, count, accumulate, start)  43 us
  transfers between devices with their start and end apart: 66, of which 64 were waited for; matrix products, arithmetic and copies ran while one was open for 13% of the time, Pallas kernels for 0%

commit v1 on v0

--- a/solution.py
+++ b/solution.py
@@ -75,7 +75,12 @@
     col_ids = jnp.arange(B, dtype=jnp.int32)[None, :]
     on_diagonal = (row_ids < per_device) & (col_ids == device_pos * per_device + row_ids)
     cover = columns + jnp.where(on_diagonal, 1.0, 0.0).astype(jnp.float32)
-    whole_rows = lax.all_to_all(prior_factor, "panel", split_axis=0, concat_axis=1, tiled=True)
+    whole_rows = jnp.concatenate(
+        lax.all_to_all(
+            jnp.stack(jnp.split(prior_factor, lax.axis_size("panel"), axis=0)), "panel", 0, 0
+        ),
+        axis=1,
+    )
     panel_prior = lax.all_gather(whole_rows[:per_device], ("row", "panel"), axis=0, tiled=True)
     update = jnp.dot(
         whole_rows,

time: 1350 us -> 1350 us (level)
    unnamed x18 -> x21, local copies, waits for them, and re-layouts: 25.7 us -> 27.3 us
where the time goes in v1:
time: 1350 us; the launch traced here: 1340 us
  waiting for transfers between devices  722 us (53%)
  other arithmetic  418 us (31%)
  local copies, waits for them, and re-layouts  69.9 us (5%)
  matrix products  55.5 us (4%)
  loops' own time  45.9 us (3%)
  between operations  19.1 us (1%)
    all_gather x1, waiting for transfers between devices, local(): lax.all_gather(schur[:per_device], ('row', 'panel'), axis=0, tiled=True)  412 us
    ppermute x63, waiting for transfers between devices, from_behind(): return lax.ppermute(block, axis, route)  283 us
    another operation x31, other arithmetic, local(): diag_factor = jnp.linalg.cholesky(diag_rows)  173 us
    reduce_sum x1024, other arithmetic, accumulate(): jnp.sum(jnp.exp(-(apart_east * apart_east + apart_north * apart_north) *...  148 us
    another operation x3, other arithmetic, local(): lax.linalg.triangular_solve(diag_factor, schur, left_side=False, lower=Tr...  83.7 us
    another operation x64, loops' own time, cover_tile(): total = lax.fori_loop(0, count, accumulate, start)  43 us
    unnamed x21, local copies, waits for them, and re-layouts  27.3 us
  transfers between devices with their start and end apart: 66, of which 64 were waited for; matrix products, arithmetic and copies ran while one was open for 13% of the time, Pallas kernels for 0%

profile of v1, /device:TPU:32, one launch (start us, length us, event | category | flops | bytes accessed | tf_op | source)
XLA Modules:
  0.0 1341.0 jit_solution(14373275677530595824)
XLA Ops:
  15.3 26.9 %all-to-all-done = f32[4,256,512]{1,2,0:T(8,128)S(1)} async-done(((f32[4,256,512]{1,2,0:T(8,128)}), f32[4,256,512]{1,2,0:T(8,128)S(1)}, u32[]{:S(2)}, u32[]{:S(2)}) %all-to-all-start) | async-done | bytes 2097184 | tf_op jit(solution)/shard_map/all_to_all | solution.py:79
  43.4 497.6 %while.68 = (s32[]{:T(128)}, f32[2,16,16]{2,1,0:T(8,128)S(1)}, f32[256,1024]{0,1:T(8,128)S(1)}, f32[16,256]{1,0:T(8,128)S(1)}, f32[16,256]{1,0:T(8,128)S(1)}, /*...) while((s32[]{:T(128)}, f32[2,16,16]{2,1,0:T(8,128)S(1)}, ...), condition=%wide.region_4.5_spmd, body=%wide.region_0.4_spmd.sunk | while | flops 466965 | bytes 123403 | solution.py:71
  548.3 10.0 reshape.143
  558.4 16.1 %convolution_subtract_fusion = f32[256,1024]{1,0:T(8,128)S(1)} fusion(f32[256,2048]{0,1:T(8,128)S(1)} %bitcast.155, f32[1024,2048]{1,0:T(8,128)} %reshape.143, f32[256,1024]{1,0:T(8,128)S(1)} %dynamic_update_slice.13, s32[256]{0:T(256)S(1)} %iota_add_fusion, pred[256]{0:T(512)(128)(4,1)S(1)} %iota_compare_fusion.4), kind=kOutput, calls=%fused_computation.16 | convolution fusion | flops 6443761664 | bytes 12584192 | tf_op jit(solution)/shard_map/dot_general | solution.py:85
  576.0 412.5 %all-gather.7.cloned.1.call-done = f32[256,4,1024]{2,1,0:T(4,128)} async-done(((f32[1,4,1024]{2,1,0:T(4,128)}), f32[256,4,1024]{2,1,0:T(4,128)}) %all-gather.7.cloned.1.call-update) | async-done | bytes 4194320 | tf_op jit(solution)/shard_map/all_gather | solution.py:92
  988.5 5.3 reshape.145
  993.8 5.8 copy.93
  1005.9 11.7 cholesky.223
  1020.2 9.8 custom-call.62
  1033.9 11.9 cholesky.244
  1046.5 9.8 custom-call.63
  1059.6 11.7 cholesky.468
  1072.0 9.8 custom-call.64
  1085.3 11.9 cholesky.487
  1097.8 9.8 custom-call.65
  1111.1 11.7 cholesky.506
  1123.5 10.2 custom-call.66
  1137.0 11.7 cholesky.526
  1149.3 9.8 custom-call.67
  1162.1 11.7 cholesky.546
  1174.5 9.8 custom-call.68
  1186.9 11.7 cholesky.564
  1214.5 22.8 %while.69 = (s32[]{:T(128)}, f32[1024,1024]{1,0:T(8,128)}, s32[8,2]{0,1:T(2,128)S(1)}, f32[8,128,128]{2,1,0:T(8,128)S(1)}, s32[]{:T(128)}) while((s32[]{:T(128)}, f32[1024,1024]{1,0:T(8,128)}, s32[8,2]{0,1:T(2,128)S(1)}, f32[8,128,128]{2,1,0:T(8,128)S(1)}, s32[]{:T(128)}) %tuple.179), condition=%wide.while_cond, body=%wide.while_body.sunk | while | flops 2 | bytes 131189 | solution.py:94
  1237.3 78.8 %custom-call.69 = f32[8,128,128]{1,2,0:T(8,128)S(1)} custom-call(f32[8,128,128]{2,1,0:T(8,128)S(1)} %get-tuple-element.405), custom_call_target="InvertDiagBlocksLowerTriangular" | custom-call | tf_op jit(solution)/shard_map/triangular_solve | solution.py:94
  (3641 shorter events, 766.1 us)
Async XLA Ops:
  10.6 31.7 %all-to-all-start = ((f32[4,256,512]{1,2,0:T(8,128)}), f32[4,256,512]{1,2,0:T(8,128)S(1)}, u32[]{:S(2)}, u32[]{:S(2)}) async-start(f32[4,256,512]{1,2,0:T(8,128)} %pad_maximum_fusion), calls=%async_computation | async-start | bytes 4194304 | tf_op jit(solution)/shard_map/all_to_all | solution.py:79
  15.0 533.3 %all-gather.5.cloned.1.call-start = ((), (), s32[]{:S(2)}) async-start(), calls=%async_computation.1 | async-start | bytes 8421376 | tf_op jit(solution)/shard_map/all_gather | solution.py:84
  43.3 945.2 %all-gather.7.cloned.1.call-start = ((), (), s32[]{:S(2)}) async-start(), calls=%async_computation.2 | async-start | bytes 4210688 | tf_op jit(solution)/shard_map/all_gather | solution.py:92
  55.2 8.0 collective-permute-start
  63.2 8.0 collective-permute-start
  71.1 8.0 collective-permute-start
  79.2 8.0 collective-permute-start
  87.2 8.1 collective-permute-start
  103.2 8.0 collective-permute-start
  119.1 8.0 collective-permute-start
  135.0 8.0 collective-permute-start
  166.8 8.0 collective-permute-start
  190.7 8.0 collective-permute-start
  198.7 8.0 collective-permute-start
  222.6 8.0 collective-permute-start
  238.5 8.0 collective-permute-start
  254.4 8.0 collective-permute-start
  278.3 8.0 collective-permute-start
  310.1 8.0 collective-permute-start
  334.0 8.0 collective-permute-start
  349.9 8.0 collective-permute-start
  397.7 8.0 collective-permute-start
  469.4 8.0 collective-permute-start
  501.2 8.0 collective-permute-start
  (48 other events, 452.1 us)
Sparse Core Ops, SparseCore 0:
  43.4 420.7 all-gather.4
  576.1 412.3 all-gather.6
